TPU v7x, 128 devices: a whole 4x4x4 slice. The times are simulated.
128 devices in a mesh: rep: 2 (over core), row: 64 (over x, z, y).
Axes of the slice: x: 4, y: 4, z: 4, core: 2. Of those that a mesh axis runs over, the one named last changes fastest.
Arguments:
- tiles: bfloat16 [512, 16, 128, 128], P('row', 'rep'), as said below
- tile_cols: int32 [512, 16], replicated, may hold values from -1 to 511, as said below
Outputs:
- vertex_counts: float32 [512, 128], P('row', 'rep')
Inputs may be any that keep to these rules, and one draw needn't show every extreme that they name: `tile_cols`: in each tile row I the filled slots come first and hold distinct tile columns from I - 32 to I, in increasing order; empty slots hold -1. At most 16 slots of a row are filled, and some row has all 16 filled. `tiles`: tiles of empty slots are zero; a tile on the diagonal (column equal to row) is zero on and above its own diagonal.
All inputs are finite; a program needn't handle non-finite values.
Results may differ from a plain program's by a relative error of at most 0.0003.
Values may be sent and summed in bfloat16 or wider, within the bound.
A program may use at most 128 MiB of HBM per device.

v0:
```python
import jax
import jax.numpy as jnp
from jax import lax
from jax.sharding import PartitionSpec as P

BACK = 4


def from_partner(x, axis, distance):
    return lax.ppermute(x, axis, [(i, i ^ 1 << distance) for i in range(lax.axis_size(axis))])


def shifted(block, axis, distance):
    devices = range(lax.axis_size(axis))
    route = [(i - distance, i) for i in devices if i - distance in devices]
    return lax.ppermute(block, axis, route)


def split_up(x, dim, devices):
    shape = x.shape
    parts = x.reshape(*shape[:dim], devices, shape[dim] // devices, *shape[dim + 1 :])
    return jnp.moveaxis(parts, dim, 0)


def sum_at_owner(x, axis, dim):
    devices = lax.axis_size(axis)
    parts = lax.all_to_all(split_up(x, dim, devices), axis, 0, 0, tiled=True)
    return jnp.sum(parts, axis=0)


def row_counts(pool, tile_cols, base, slot_start, width):
    pool_rows = pool.shape[0]

    def one_row(item):
        whole_row, cols = item
        local = jnp.clip(cols - base, 0, pool_rows - 1)
        panels = jnp.take(pool, local, axis=0)
        safe = jnp.maximum(cols, 0)
        named = jnp.take(tile_cols, safe, axis=0)
        panel_cols = lax.dynamic_slice_in_dim(named, slot_start, width, 1)
        match = (panel_cols[:, :, None] == cols[None, None, :]) & (cols >= 0)[None, None, :]
        masks = jnp.einsum(
            "kjp,pac->kjac",
            match.astype(jnp.bfloat16),
            whole_row,
            preferred_element_type=jnp.float32,
        ).astype(jnp.bfloat16)
        product = jnp.einsum(
            "kab,kjbc->kjac", whole_row, panels, preferred_element_type=jnp.float32
        )
        return jnp.sum(product * masks.astype(jnp.float32), axis=(0, 1, 3))

    return one_row


def body(tiles, tile_cols):
    rows_here, half_slots, tile, _ = tiles.shape
    index_rep = lax.axis_index("rep")
    index_row = lax.axis_index("row")
    partner = from_partner(tiles, "rep", 0)
    first = jnp.where(index_rep == 0, tiles, partner)
    second = jnp.where(index_rep == 0, partner, tiles)
    full = jnp.concatenate([first, second], axis=1)
    my_cols = lax.dynamic_slice_in_dim(tile_cols, index_row * rows_here, rows_here, 0)
    base = (index_row - BACK) * rows_here
    earlier = [shifted(tiles, "row", BACK - step) for step in range(BACK)]
    pool = jnp.concatenate(earlier + [tiles], axis=0)
    one_row = row_counts(pool, tile_cols, base, index_rep * half_slots, half_slots)
    partial_counts = lax.map(one_row, (full, my_cols))
    counts = sum_at_owner(partial_counts, "rep", 1)
    return counts


def solution(mesh):
    return jax.shard_map(
        body,
        mesh=mesh,
        in_specs=(P("row", "rep", None, None), P()),
        out_specs=P("row", "rep"),
        check_vma=False,
    )
```

profile of v0, /device:TPU:1, one launch (start us, length us, event | category | flops | bytes accessed | tf_op | source)
XLA Modules:
  0.0 410.4 jit_solution(2979151015411077554)
XLA Ops:
  0.0 5.7 %collective-permute-start = (bf16[8,8,128,128]{3,2,1,0:T(8,128)(2,1)}, bf16[8,8,128,128]{3,2,1,0:T(8,128)(2,1)}, u32[]{:S(2)}, u32[]{:S(2)}) collective-permute-start(bf16[8,8,128,128]{3,2,1,0:T(8,128)(2,1)} %param.4), channel_id=1, source_target_pairs={{0,4},{1,5},{2,6},{3,7},{4,8},{5,9},{6,10},{7,11},{8,12},{9,13},{1... | collective-permute-start | bytes 6291464 | tf_op jit(solution)/shard_map/ppermute | solution.py:16
  5.7 6.0 %collective-permute-start.1 = (bf16[8,8,128,128]{3,2,1,0:T(8,128)(2,1)}, bf16[8,8,128,128]{3,2,1,0:T(8,128)(2,1)}, u32[]{:S(2)}, u32[]{:S(2)}) collective-permute-start(bf16[8,8,128,128]{3,2,1,0:T(8,128)(2,1)} %param.4), channel_id=1, source_target_pairs={{0,3},{1,4},{2,5},{3,6},{4,7},{5,8},{6,9},{7,10},{8,11},{9,12},{10... | collective-permute-start | bytes 6291464 | tf_op jit(solution)/shard_map/ppermute | solution.py:16
  11.7 3.6 collective-permute-start.2
  19.5 164.3 %collective-permute-done = bf16[8,8,128,128]{3,2,1,0:T(8,128)(2,1)} collective-permute-done((bf16[8,8,128,128]{3,2,1,0:T(8,128)(2,1)}, bf16[8,8,128,128]{3,2,1,0:T(8,128)(2,1)}, u32[]{:S(2)}, u32[]{:S(2)}) %collective-permute-start) | collective-permute-done | bytes 2097184 | tf_op jit(solution)/shard_map/ppermute | solution.py:16
  194.9 4.4 %broadcast_select_fusion.1 = (bf16[8,8,128,128]{3,2,1,0:T(8,128)(2,1)S(1)}, bf16[8,8,128,128]{3,2,1,0:T(8,128)(2,1)S(1)}, bf16[40,8,128,128]{3,2,1,0:T(8,128)(2,1)}) fusion(bf16[8,8,128,128]{3,2,1,0:T(8,128)(2,1)S(1)} %copy-done, bf16[8,8,128,128]{3,2,1,0:T(8,128)(2,1)} %collective-permute-done.4, pred[]{:T(512)S(6)} %eq.24, ...), kind=kLoop, calls=%fused_computation.35 | loop fusion | flops 2097152 | bytes 10485761 | tf_op jit(solution)/shard_map/jit(_where)/select_n | solution.py:61
  201.8 201.7 %while.12 = (s32[]{:T(128)}, f32[8,128]{1,0:T(8,128)S(1)}, s32[8,16]{1,0:T(8,128)S(1)}, s32[]{:T(128)}, bf16[40,8,128,128]{3,2,1,0:T(8,128)(2,1)}, /*index=5*/bf...) while((s32[]{:T(128)}, f32[8,128]{1,0:T(8,128)S(1)}, ...), condition=%wide.region_2.3_spmd, body=%wide.region_0.2_spmd.sunk | while | flops 612374784 | bytes 31472092 | solution.py:69
  206.9 6.8 %copy.29 = bf16[16,8,128,128]{2,3,1,0:T(8,128)(2,1)} copy(bf16[16,8,128,128]{3,1,2,0:T(8,128)(2,1)} %fusion.32) | data formatting | bytes 8388608 | tf_op jit(solution)/shard_map/while/body/eval_jaxpr/kjp,pac->kjac/dot_general | solution.py:42
  213.7 7.1 %gather_fusion.1 = bf16[16,8,128,128]{3,2,1,0:T(8,128)(2,1)} fusion(bf16[40,8,128,128]{3,2,1,0:T(8,128)(2,1)} %get-tuple-element.230, s32[1024]{0:T(1024)S(1)} %pad_clamp_fusion.5), kind=kCustom, calls=%fused_computation.clone.1 | custom fusion | bytes 8388672 | tf_op jit(solution)/shard_map/while/body/eval_jaxpr/jit(_take)/gather | solution.py:37
  220.8 6.2 %fusion.34 = f32[128]{0:T(128)S(1)} fusion(bf16[16,8,128,128]{2,3,1,0:T(8,128)(2,1)} %copy.29, bf16[16,8,128,128]{3,2,1,0:T(8,128)(2,1)} %gather_fusion.1, pred[16]{0:T(512)(128)(4,1)S(1)} %get-tuple-element.205, bf16[8,16,128,128]{3,2,1,0:T(8,128)(2,1)} %get-tuple-element.231, s32[]{:T(128)} %get-tuple-element.216), kind=kOutput, calls=%fused_computation.3.clone.1 | convolution fusion | flops 545259392 | bytes 8913936 | tf_op jit(solution)/shard_map/while/body/eval_jaxpr/kab,kjbc->kjac/dot_general | solution.py:48
  232.1 6.8 %copy.29 = bf16[16,8,128,128]{2,3,1,0:T(8,128)(2,1)} copy(bf16[16,8,128,128]{3,1,2,0:T(8,128)(2,1)} %fusion.32) | data formatting | bytes 8388608 | tf_op jit(solution)/shard_map/while/body/eval_jaxpr/kjp,pac->kjac/dot_general | solution.py:42
  238.9 7.1 %gather_fusion.1 = bf16[16,8,128,128]{3,2,1,0:T(8,128)(2,1)} fusion(bf16[40,8,128,128]{3,2,1,0:T(8,128)(2,1)} %get-tuple-element.230, s32[1024]{0:T(1024)S(1)} %pad_clamp_fusion.5), kind=kCustom, calls=%fused_computation.clone.1 | custom fusion | bytes 8388672 | tf_op jit(solution)/shard_map/while/body/eval_jaxpr/jit(_take)/gather | solution.py:37
  246.0 6.2 %fusion.34 = f32[128]{0:T(128)S(1)} fusion(bf16[16,8,128,128]{2,3,1,0:T(8,128)(2,1)} %copy.29, bf16[16,8,128,128]{3,2,1,0:T(8,128)(2,1)} %gather_fusion.1, pred[16]{0:T(512)(128)(4,1)S(1)} %get-tuple-element.205, bf16[8,16,128,128]{3,2,1,0:T(8,128)(2,1)} %get-tuple-element.231, s32[]{:T(128)} %get-tuple-element.216), kind=kOutput, calls=%fused_computation.3.clone.1 | convolution fusion | flops 545259392 | bytes 8913936 | tf_op jit(solution)/shard_map/while/body/eval_jaxpr/kab,kjbc->kjac/dot_general | solution.py:48
  257.3 6.8 %copy.29 = bf16[16,8,128,128]{2,3,1,0:T(8,128)(2,1)} copy(bf16[16,8,128,128]{3,1,2,0:T(8,128)(2,1)} %fusion.32) | data formatting | bytes 8388608 | tf_op jit(solution)/shard_map/while/body/eval_jaxpr/kjp,pac->kjac/dot_general | solution.py:42
  264.1 7.1 %gather_fusion.1 = bf16[16,8,128,128]{3,2,1,0:T(8,128)(2,1)} fusion(bf16[40,8,128,128]{3,2,1,0:T(8,128)(2,1)} %get-tuple-element.230, s32[1024]{0:T(1024)S(1)} %pad_clamp_fusion.5), kind=kCustom, calls=%fused_computation.clone.1 | custom fusion | bytes 8388672 | tf_op jit(solution)/shard_map/while/body/eval_jaxpr/jit(_take)/gather | solution.py:37
  271.2 6.2 %fusion.34 = f32[128]{0:T(128)S(1)} fusion(bf16[16,8,128,128]{2,3,1,0:T(8,128)(2,1)} %copy.29, bf16[16,8,128,128]{3,2,1,0:T(8,128)(2,1)} %gather_fusion.1, pred[16]{0:T(512)(128)(4,1)S(1)} %get-tuple-element.205, bf16[8,16,128,128]{3,2,1,0:T(8,128)(2,1)} %get-tuple-element.231, s32[]{:T(128)} %get-tuple-element.216), kind=kOutput, calls=%fused_computation.3.clone.1 | convolution fusion | flops 545259392 | bytes 8913936 | tf_op jit(solution)/shard_map/while/body/eval_jaxpr/kab,kjbc->kjac/dot_general | solution.py:48
  282.5 6.8 %copy.29 = bf16[16,8,128,128]{2,3,1,0:T(8,128)(2,1)} copy(bf16[16,8,128,128]{3,1,2,0:T(8,128)(2,1)} %fusion.32) | data formatting | bytes 8388608 | tf_op jit(solution)/shard_map/while/body/eval_jaxpr/kjp,pac->kjac/dot_general | solution.py:42
  289.4 7.1 %gather_fusion.1 = bf16[16,8,128,128]{3,2,1,0:T(8,128)(2,1)} fusion(bf16[40,8,128,128]{3,2,1,0:T(8,128)(2,1)} %get-tuple-element.230, s32[1024]{0:T(1024)S(1)} %pad_clamp_fusion.5), kind=kCustom, calls=%fused_computation.clone.1 | custom fusion | bytes 8388672 | tf_op jit(solution)/shard_map/while/body/eval_jaxpr/jit(_take)/gather | solution.py:37
  296.4 6.2 %fusion.34 = f32[128]{0:T(128)S(1)} fusion(bf16[16,8,128,128]{2,3,1,0:T(8,128)(2,1)} %copy.29, bf16[16,8,128,128]{3,2,1,0:T(8,128)(2,1)} %gather_fusion.1, pred[16]{0:T(512)(128)(4,1)S(1)} %get-tuple-element.205, bf16[8,16,128,128]{3,2,1,0:T(8,128)(2,1)} %get-tuple-element.231, s32[]{:T(128)} %get-tuple-element.216), kind=kOutput, calls=%fused_computation.3.clone.1 | convolution fusion | flops 545259392 | bytes 8913936 | tf_op jit(solution)/shard_map/while/body/eval_jaxpr/kab,kjbc->kjac/dot_general | solution.py:48
  307.8 6.8 %copy.29 = bf16[16,8,128,128]{2,3,1,0:T(8,128)(2,1)} copy(bf16[16,8,128,128]{3,1,2,0:T(8,128)(2,1)} %fusion.32) | data formatting | bytes 8388608 | tf_op jit(solution)/shard_map/while/body/eval_jaxpr/kjp,pac->kjac/dot_general | solution.py:42
  314.6 7.1 %gather_fusion.1 = bf16[16,8,128,128]{3,2,1,0:T(8,128)(2,1)} fusion(bf16[40,8,128,128]{3,2,1,0:T(8,128)(2,1)} %get-tuple-element.230, s32[1024]{0:T(1024)S(1)} %pad_clamp_fusion.5), kind=kCustom, calls=%fused_computation.clone.1 | custom fusion | bytes 8388672 | tf_op jit(solution)/shard_map/while/body/eval_jaxpr/jit(_take)/gather | solution.py:37
  321.7 6.2 %fusion.34 = f32[128]{0:T(128)S(1)} fusion(bf16[16,8,128,128]{2,3,1,0:T(8,128)(2,1)} %copy.29, bf16[16,8,128,128]{3,2,1,0:T(8,128)(2,1)} %gather_fusion.1, pred[16]{0:T(512)(128)(4,1)S(1)} %get-tuple-element.205, bf16[8,16,128,128]{3,2,1,0:T(8,128)(2,1)} %get-tuple-element.231, s32[]{:T(128)} %get-tuple-element.216), kind=kOutput, calls=%fused_computation.3.clone.1 | convolution fusion | flops 545259392 | bytes 8913936 | tf_op jit(solution)/shard_map/while/body/eval_jaxpr/kab,kjbc->kjac/dot_general | solution.py:48
  333.0 6.8 %copy.29 = bf16[16,8,128,128]{2,3,1,0:T(8,128)(2,1)} copy(bf16[16,8,128,128]{3,1,2,0:T(8,128)(2,1)} %fusion.32) | data formatting | bytes 8388608 | tf_op jit(solution)/shard_map/while/body/eval_jaxpr/kjp,pac->kjac/dot_general | solution.py:42
  339.8 7.1 %gather_fusion.1 = bf16[16,8,128,128]{3,2,1,0:T(8,128)(2,1)} fusion(bf16[40,8,128,128]{3,2,1,0:T(8,128)(2,1)} %get-tuple-element.230, s32[1024]{0:T(1024)S(1)} %pad_clamp_fusion.5), kind=kCustom, calls=%fused_computation.clone.1 | custom fusion | bytes 8388672 | tf_op jit(solution)/shard_map/while/body/eval_jaxpr/jit(_take)/gather | solution.py:37
  346.9 6.2 %fusion.34 = f32[128]{0:T(128)S(1)} fusion(bf16[16,8,128,128]{2,3,1,0:T(8,128)(2,1)} %copy.29, bf16[16,8,128,128]{3,2,1,0:T(8,128)(2,1)} %gather_fusion.1, pred[16]{0:T(512)(128)(4,1)S(1)} %get-tuple-element.205, bf16[8,16,128,128]{3,2,1,0:T(8,128)(2,1)} %get-tuple-element.231, s32[]{:T(128)} %get-tuple-element.216), kind=kOutput, calls=%fused_computation.3.clone.1 | convolution fusion | flops 545259392 | bytes 8913936 | tf_op jit(solution)/shard_map/while/body/eval_jaxpr/kab,kjbc->kjac/dot_general | solution.py:48
  354.9 3.3 fusion.32
  358.2 6.8 %copy.29 = bf16[16,8,128,128]{2,3,1,0:T(8,128)(2,1)} copy(bf16[16,8,128,128]{3,1,2,0:T(8,128)(2,1)} %fusion.32) | data formatting | bytes 8388608 | tf_op jit(solution)/shard_map/while/body/eval_jaxpr/kjp,pac->kjac/dot_general | solution.py:42
  365.0 7.1 %gather_fusion.1 = bf16[16,8,128,128]{3,2,1,0:T(8,128)(2,1)} fusion(bf16[40,8,128,128]{3,2,1,0:T(8,128)(2,1)} %get-tuple-element.230, s32[1024]{0:T(1024)S(1)} %pad_clamp_fusion.5), kind=kCustom, calls=%fused_computation.clone.1 | custom fusion | bytes 8388672 | tf_op jit(solution)/shard_map/while/body/eval_jaxpr/jit(_take)/gather | solution.py:37
  372.1 6.2 %fusion.34 = f32[128]{0:T(128)S(1)} fusion(bf16[16,8,128,128]{2,3,1,0:T(8,128)(2,1)} %copy.29, bf16[16,8,128,128]{3,2,1,0:T(8,128)(2,1)} %gather_fusion.1, pred[16]{0:T(512)(128)(4,1)S(1)} %get-tuple-element.205, bf16[8,16,128,128]{3,2,1,0:T(8,128)(2,1)} %get-tuple-element.231, s32[]{:T(128)} %get-tuple-element.216), kind=kOutput, calls=%fused_computation.3.clone.1 | convolution fusion | flops 545259392 | bytes 8913936 | tf_op jit(solution)/shard_map/while/body/eval_jaxpr/kab,kjbc->kjac/dot_general | solution.py:48
  383.4 6.8 %copy.29 = bf16[16,8,128,128]{2,3,1,0:T(8,128)(2,1)} copy(bf16[16,8,128,128]{3,1,2,0:T(8,128)(2,1)} %fusion.32) | data formatting | bytes 8388608 | tf_op jit(solution)/shard_map/while/body/eval_jaxpr/kjp,pac->kjac/dot_general | solution.py:42
  390.2 7.1 %gather_fusion.1 = bf16[16,8,128,128]{3,2,1,0:T(8,128)(2,1)} fusion(bf16[40,8,128,128]{3,2,1,0:T(8,128)(2,1)} %get-tuple-element.230, s32[1024]{0:T(1024)S(1)} %pad_clamp_fusion.5), kind=kCustom, calls=%fused_computation.clone.1 | custom fusion | bytes 8388672 | tf_op jit(solution)/shard_map/while/body/eval_jaxpr/jit(_take)/gather | solution.py:37
  397.3 6.2 %fusion.34 = f32[128]{0:T(128)S(1)} fusion(bf16[16,8,128,128]{2,3,1,0:T(8,128)(2,1)} %copy.29, bf16[16,8,128,128]{3,2,1,0:T(8,128)(2,1)} %gather_fusion.1, pred[16]{0:T(512)(128)(4,1)S(1)} %get-tuple-element.205, bf16[8,16,128,128]{3,2,1,0:T(8,128)(2,1)} %get-tuple-element.231, s32[]{:T(128)} %get-tuple-element.216), kind=kOutput, calls=%fused_computation.3.clone.1 | convolution fusion | flops 545259392 | bytes 8913936 | tf_op jit(solution)/shard_map/while/body/eval_jaxpr/kab,kjbc->kjac/dot_general | solution.py:48
  403.7 4.9 %all_to_all.5 = f32[2,1,512]{2,1,0:T(1,128)S(1)} all-to-all(f32[2,1,512]{2,1,0:T(1,128)S(1)} %reshape.92), channel_id=1, replica_groups=mesh['rep'=2,'row'=64] {'rep'}, dimensions={0} | all-to-all | bytes 8192 | tf_op jit(solution)/shard_map/all_to_all | solution.py:27
  (110 shorter events, 57.4 us)
Async XLA Ops:
  0.0 183.8 %collective-permute-start = (bf16[8,8,128,128]{3,2,1,0:T(8,128)(2,1)}, bf16[8,8,128,128]{3,2,1,0:T(8,128)(2,1)}, u32[]{:S(2)}, u32[]{:S(2)}) collective-permute-start(bf16[8,8,128,128]{3,2,1,0:T(8,128)(2,1)} %param.4), channel_id=1, source_target_pairs={{0,4},{1,5},{2,6},{3,7},{4,8},{5,9},{6,10},{7,11},{8,12},{9,13},{1... | collective-permute-start | bytes 6291464 | tf_op jit(solution)/shard_map/ppermute | solution.py:16
  5.7 181.3 %collective-permute-start.1 = (bf16[8,8,128,128]{3,2,1,0:T(8,128)(2,1)}, bf16[8,8,128,128]{3,2,1,0:T(8,128)(2,1)}, u32[]{:S(2)}, u32[]{:S(2)}) collective-permute-start(bf16[8,8,128,128]{3,2,1,0:T(8,128)(2,1)} %param.4), channel_id=1, source_target_pairs={{0,3},{1,4},{2,5},{3,6},{4,7},{5,8},{6,9},{7,10},{8,11},{9,12},{10... | collective-permute-start | bytes 6291464 | tf_op jit(solution)/shard_map/ppermute | solution.py:16
  11.7 178.5 %collective-permute-start.2 = (bf16[8,8,128,128]{3,2,1,0:T(8,128)(2,1)}, bf16[8,8,128,128]{3,2,1,0:T(8,128)(2,1)}, u32[]{:S(2)}, u32[]{:S(2)}) collective-permute-start(bf16[8,8,128,128]{3,2,1,0:T(8,128)(2,1)} %param.4), channel_id=1, source_target_pairs={{0,2},{1,3},{2,4},{3,5},{4,6},{5,7},{6,8},{7,9},{8,10},{9,11},{10,... | collective-permute-start | bytes 6291464 | tf_op jit(solution)/shard_map/ppermute | solution.py:16
  15.3 178.2 %collective-permute-start.3 = (bf16[8,8,128,128]{3,2,1,0:T(8,128)(2,1)}, bf16[8,8,128,128]{3,2,1,0:T(8,128)(2,1)S(1)}, u32[]{:S(2)}, u32[]{:S(2)}) collective-permute-start(bf16[8,8,128,128]{3,2,1,0:T(8,128)(2,1)} %param.4), channel_id=1, source_target_pairs={{0,1},{1,2},{2,3},{3,4},{4,5},{5,6},{6,7},{7,8},{8,9},{9,10},{10,1... | collective-permute-start | bytes 6291464 | tf_op jit(solution)/shard_map/ppermute | solution.py:16
  16.7 178.2 %collective-permute-start.4 = (bf16[8,8,128,128]{3,2,1,0:T(8,128)(2,1)}, bf16[8,8,128,128]{3,2,1,0:T(8,128)(2,1)}, u32[]{:S(2)}, u32[]{:S(2)}) collective-permute-start(bf16[8,8,128,128]{3,2,1,0:T(8,128)(2,1)} %param.4), channel_id=1, source_target_pairs={{0,64},{64,0},{1,65},{65,1},{2,66},{66,2},{3,67},{67,3},{4,68},{68... | collective-permute-start | bytes 6291464 | tf_op jit(solution)/shard_map/ppermute | solution.py:10
  190.1 4.8 %copy-start = (bf16[8,8,128,128]{3,2,1,0:T(8,128)(2,1)S(1)}, bf16[8,8,128,128]{3,2,1,0:T(8,128)(2,1)}, u32[]{:S(2)}) copy-start(bf16[8,8,128,128]{3,2,1,0:T(8,128)(2,1)} %param.4) | copy-start | bytes 6291460
where the time goes:
time: 412 us; the launch traced here: 410 us
  waiting for transfers between devices  164 us (40%)
  local copies, waits for them, and re-layouts  137 us (33%)
  matrix products  75.9 us (18%)
  starting transfers between devices  18.6 us (5%)
  other arithmetic  9.17 us (2%)
  blocking collectives  4.87 us (1%)
    ppermute x4, waiting for transfers between devices, shifted(): return lax.ppermute(block, axis, route)  164 us
    gather x8, local copies, waits for them, and re-layouts, one_row(): panels = jnp.take(pool, local, axis=0)  56.7 us
    dot_general x8, local copies, waits for them, and re-layouts, one_row(): jnp.einsum('kjp,pac->kjac', match.astype(jnp.bfloat16), whole_row, prefer...  54.4 us
    dot_general x8, matrix products, one_row(): jnp.einsum('kab,kjbc->kjac', whole_row, panels, preferred_element_type=jn...  49.3 us
    dot_general x8, matrix products, one_row(): jnp.einsum('kjp,pac->kjac', match.astype(jnp.bfloat16), whole_row, prefer...  26.5 us
    ppermute x4, starting transfers between devices, shifted(): return lax.ppermute(block, axis, route)  16.7 us
    unnamed x9, local copies, waits for them, and re-layouts  12.1 us
    squeeze x8, local copies, waits for them, and re-layouts, body(): partial_counts = lax.map(one_row, (full, my_cols))  8.62 us
  transfers between devices with their start and end apart: 5, of which 1 were waited for; matrix products, arithmetic and copies ran while one was open for 3% of the time, Pallas kernels for 0%

commit v1 on v0

v1 whole, which is shorter than its diff:
```python
import functools

import jax
import jax.numpy as jnp
from jax import lax
from jax.experimental import pallas as pl
from jax.experimental.pallas import tpu as pltpu
from jax.sharding import PartitionSpec as P

MESH = pl.DeviceIdType.MESH
ROWS = 8
HALF = 8
SLOTS = 16
NONE = ROWS * SLOTS
DIST = 4
PAIRS = ((0, 0), (0, -1), (0, -DIST), (1, -1), (-1, -DIST))


def lookup_table(tile_cols, rep, row, blocks):
    cols = {
        d: lax.dynamic_slice_in_dim(
            tile_cols, lax.rem(row + d + blocks, blocks) * ROWS, ROWS, 0
        )
        for d in (0, -1, 1, -DIST)
    }
    place = (jnp.arange(ROWS)[:, None] * SLOTS + jnp.arange(SLOTS)[None, :]).astype(jnp.int32)
    tables = []
    for block_i, block_k in PAIRS:
        named = lax.dynamic_slice_in_dim(cols[block_k], rep * HALF, HALF, 1)
        own = lax.rem(row + block_k + blocks, blocks) * ROWS + jnp.arange(ROWS)
        wanted = jnp.concatenate([own[:, None].astype(jnp.int32), named], axis=1)
        same = (wanted[:, None, :, None] == cols[block_i][None, :, None, :]) & (
            wanted >= 0
        )[:, None, :, None]
        found = jnp.max(jnp.where(same, place[None, :, None, :], -1), axis=-1)
        tables.append(jnp.where(found < 0, NONE, found))
    return jnp.stack(tables).reshape(len(PAIRS) * ROWS, ROWS * (1 + HALF))


def kernel(
    blocks,
    table,
    tiles,
    out,
    own,
    before,
    after,
    far,
    acc,
    given,
    got,
    local_sem,
    pair_send,
    pair_recv,
    far_send,
    far_recv,
    before_send,
    before_recv,
    after_send,
    after_recv,
    pass_before_send,
    pass_before_recv,
    pass_after_send,
    pass_after_recv,
    sum_send,
    sum_recv,
):
    rep = lax.axis_index("rep")
    row = lax.axis_index("row")
    other = 1 - rep
    y = lax.rem(row, DIST)
    last_y = y == DIST - 1
    first_y = y == 0

    def at(step):
        return lax.rem(row + step + blocks, blocks)

    barrier = pltpu.get_barrier_semaphore()

    def greet(device):
        pl.semaphore_signal(barrier, inc=1, device_id=device, device_id_type=MESH)

    greet((other, row))
    for step in (1, -1):
        greet((rep, at(step)))
        greet((other, at(step)))
    for step in (DIST, -DIST):
        greet((rep, at(step)))

    @pl.when(last_y)
    def _():
        greet((rep, at(1 - DIST)))

    @pl.when(first_y)
    def _():
        greet((rep, at(DIST - 1)))

    def mine(c, count=HALF, skip=0):
        return pl.ds(c * SLOTS + rep * HALF + skip, count)

    def load(c):
        return pltpu.make_async_copy(tiles.at[c], own.at[mine(c)], local_sem.at[c])

    def to_partner(c):
        return pltpu.make_async_remote_copy(
            tiles.at[c], own.at[mine(c)], pair_send.at[c], pair_recv.at[c],
            device_id=(other, row), device_id_type=MESH,
        )

    def to_far(c, h):
        return pltpu.make_async_remote_copy(
            tiles.at[c, pl.ds(h * 4, 4)], far.at[c, pl.ds(h * 4, 4)],
            far_send.at[2 * c + h], far_recv.at[2 * c + h],
            device_id=(rep, at(DIST)), device_id_type=MESH,
        )

    def to_next(c, h):
        return pltpu.make_async_remote_copy(
            tiles.at[c, pl.ds(h * 4, 4)], before.at[mine(c, 4, h * 4)],
            before_send.at[2 * c + h], before_recv.at[2 * c + h],
            device_id=(rep, at(1)), device_id_type=MESH,
        )

    def relay(c, h):
        return pltpu.make_async_remote_copy(
            far.at[c, pl.ds(h * 4, 4)], before.at[mine(c, 4, h * 4)],
            before_send.at[2 * c + h], before_recv.at[2 * c + h],
            device_id=(rep, at(1 - DIST)), device_id_type=MESH,
        )

    def to_previous(c):
        return pltpu.make_async_remote_copy(
            tiles.at[c], after.at[mine(c)], after_send.at[c], after_recv.at[c],
            device_id=(rep, at(-1)), device_id_type=MESH,
        )

    def pass_before(c):
        return pltpu.make_async_remote_copy(
            before.at[mine(c)], before.at[mine(c)],
            pass_before_send.at[c], pass_before_recv.at[c],
            device_id=(other, row), device_id_type=MESH,
        )

    def pass_after(c):
        return pltpu.make_async_remote_copy(
            after.at[mine(c)], after.at[mine(c)],
            pass_after_send.at[c], pass_after_recv.at[c],
            device_id=(other, row), device_id_type=MESH,
        )

    for c in range(ROWS):
        load(c).start()
    zero = jnp.zeros((128, 128), jnp.bfloat16)
    for ref in (own, before, after):
        ref[NONE] = zero
    acc[...] = jnp.zeros_like(acc)

    edge = jnp.logical_or(first_y, last_y).astype(jnp.int32)
    pl.semaphore_wait(barrier, 7 + edge)

    @pl.loop(0, ROWS)
    def _(c):
        for h in range(2):
            to_far(c, h).start()

            @pl.when(jnp.logical_not(last_y))
            def _():
                to_next(c, h).start()

        to_previous(c).start()
        to_partner(c).start()

    @pl.loop(0, ROWS)
    def _(c):
        load(c).wait()
        to_partner(c).wait()

    def combine(pair, rows_i, tiles_k, total, c):
        right = jnp.concatenate(tiles_k, axis=1)
        for i in range(ROWS):
            at_i = i * (1 + HALF)
            left = rows_i[table[pair * ROWS + c, at_i]]
            product = jnp.dot(left, right, preferred_element_type=jnp.float32)
            here = acc[total * ROWS + i]
            for s in range(HALF):
                weight = rows_i[table[pair * ROWS + c, at_i + 1 + s]]
                here += product[:, s * 128 : s * 128 + 128] * weight.astype(jnp.float32)
            acc[total * ROWS + i] = here

    def half_row(ref, c):
        return [ref[c * SLOTS + rep * HALF + s] for s in range(HALF)]

    @pl.loop(0, ROWS)
    def _(c):
        for h in range(2):
            to_far(c, h).wait_recv()

            @pl.when(last_y)
            def _():
                relay(c, h).start()

        to_previous(c).wait_recv()
        pass_after(c).start()
        for h in range(2):
            to_next(c, h).wait_recv()
        pass_before(c).start()
        combine(0, own, half_row(own, c), 0, c)
        combine(2, own, [far[c, s] for s in range(HALF)], 0, c)
        combine(1, own, half_row(before, c), 0, c)

    @pl.loop(0, ROWS)
    def _(c):
        pass_after(c).wait()
        pass_before(c).wait()

    @pl.loop(0, ROWS)
    def _(c):
        combine(3, after, half_row(before, c), 1, c)
        combine(4, before, [far[c, s] for s in range(HALF)], 2, c)

    for t in range(3):
        given[t] = jnp.sum(acc[t * ROWS : t * ROWS + ROWS], axis=-1)

    sums = []
    for slot, (source, device) in enumerate(
        (
            (0, (other, row)),
            (1, (rep, at(1))),
            (1, (other, at(1))),
            (2, (rep, at(-1))),
            (2, (other, at(-1))),
        )
    ):
        sums.append(
            pltpu.make_async_remote_copy(
                given.at[source], got.at[slot], sum_send.at[slot], sum_recv.at[slot],
                device_id=device, device_id_type=MESH,
            )
        )
    for copy in sums:
        copy.start()
    for copy in sums:
        copy.wait()
    total = given[0]
    for slot in range(5):
        total += got[slot]
    out[...] = jnp.where(rep == 0, total[:, :64], total[:, 64:])

    @pl.loop(0, ROWS)
    def _(c):
        for h in range(2):
            to_far(c, h).wait_send()
            to_next(c, h).wait_send()
        to_previous(c).wait_send()


def body(blocks, tiles, tile_cols):
    rep = lax.axis_index("rep")
    row = lax.axis_index("row")
    table = lookup_table(tile_cols, rep, row, blocks)
    dma = pltpu.SemaphoreType.DMA
    tile = (128, 128)
    return pl.pallas_call(
        functools.partial(kernel, blocks),
        out_shape=jax.ShapeDtypeStruct((ROWS, 64), jnp.float32),
        in_specs=[
            pl.BlockSpec(memory_space=pltpu.SMEM),
            pl.BlockSpec(memory_space=pltpu.HBM),
        ],
        out_specs=pl.BlockSpec(memory_space=pltpu.VMEM),
        scratch_shapes=[
            pltpu.VMEM((NONE + 1, *tile), jnp.bfloat16),
            pltpu.VMEM((NONE + 1, *tile), jnp.bfloat16),
            pltpu.VMEM((NONE + 1, *tile), jnp.bfloat16),
            pltpu.VMEM((ROWS, HALF, *tile), jnp.bfloat16),
            pltpu.VMEM((3 * ROWS, *tile), jnp.float32),
            pltpu.VMEM((3, ROWS, 128), jnp.float32),
            pltpu.VMEM((5, ROWS, 128), jnp.float32),
            dma((ROWS,)),
            dma((ROWS,)),
            dma((ROWS,)),
            dma((2 * ROWS,)),
            dma((2 * ROWS,)),
            dma((2 * ROWS,)),
            dma((2 * ROWS,)),
            dma((ROWS,)),
            dma((ROWS,)),
            dma((ROWS,)),
            dma((ROWS,)),
            dma((ROWS,)),
            dma((ROWS,)),
            dma((5,)),
            dma((5,)),
        ],
        compiler_params=pltpu.CompilerParams(
            collective_id=0, has_side_effects=True, vmem_limit_bytes=40 << 20
        ),
        name="triangles",
    )(table, tiles)


def solution(mesh):
    return jax.shard_map(
        functools.partial(body, mesh.shape["row"]),
        mesh=mesh,
        in_specs=(P("row", "rep", None, None), P()),
        out_specs=P("row", "rep"),
        check_vma=False,
    )
```

time: 412 us -> 91.6 us (0.22)
  waiting for transfers between devices: 164 us -> 0 us
  local copies, waits for them, and re-layouts: 137 us -> 4.71 us
  Pallas kernels: 0 us -> 79.4 us
  matrix products: 75.9 us -> 0 us
  starting transfers between devices: 18.6 us -> 0 us
  blocking collectives: 4.87 us -> 0 us
    ppermute x5 -> x0, waiting for transfers between devices: 164 us -> none  [the longest x4 164 us: shifted(): return lax.ppermute(block, axis, route)]
    pallas_call x0 -> x1, Pallas kernels: none -> 79.4 us  [body(): pl.pallas_call(functools.partial(kernel, blocks), out_shape=jax.ShapeDtyp...]
    dot_general x16 -> x0, matrix products: 75.9 us -> none  [the longest x8 49.3 us: one_row(): jnp.einsum('kab,kjbc->kjac', whole_row, panels, preferred_element_type=jn...]
    gather x16 -> x0, local copies, waits for them, and re-layouts: 61.2 us -> none  [the longest x8 56.7 us: one_row(): panels = jnp.take(pool, local, axis=0)]
    dot_general x8 -> x0, local copies, waits for them, and re-layouts: 54.4 us -> none  [one_row(): jnp.einsum('kjp,pac->kjac', match.astype(jnp.bfloat16), whole_row, prefer...]
    ppermute x5 -> x0, starting transfers between devices: 18.6 us -> none  [the longest x4 16.7 us: shifted(): return lax.ppermute(block, axis, route)]
    unnamed x9 -> x6, local copies, waits for them, and re-layouts: 12.1 us -> 2.39 us
    squeeze x8 -> x0, local copies, waits for them, and re-layouts: 8.62 us -> none  [body(): partial_counts = lax.map(one_row, (full, my_cols))]
  transfers between devices with their start and end apart: 5 -> 0, of which waited for: 1 -> 0; matrix products, arithmetic and copies ran while one was open for 3% -> 0% of each run, Pallas kernels for 0% -> 0%
where the time goes in v1:
time: 91.6 us; the launch traced here: 91.4 us
  Pallas kernels  79.4 us (87%)
  other arithmetic  7.15 us (8%)
  local copies, waits for them, and re-layouts  4.71 us (5%)
    pallas_call x1, Pallas kernels, body(): pl.pallas_call(functools.partial(kernel, blocks), out_shape=jax.ShapeDtyp...  79.4 us
    reduce_max x1, other arithmetic, lookup_table(): found = jnp.max(jnp.where(same, place[None, :, None, :], -1), axis=-1)  6.86 us
    unnamed x6, local copies, waits for them, and re-layouts  2.39 us

profile of v1, /device:TPU:1, one launch (start us, length us, event | category | flops | bytes accessed | tf_op | source)
XLA Modules:
  0.0 91.4 jit_solution(5704228758922005194)
XLA Ops:
  0.0 0.1 iota_add_fusion.2
  0.1 0.9 fusion.5
  1.0 0.1 copy.29
  1.0 0.1 broadcast_compare_fusion.2
  1.1 0.1 copy.30
  1.2 0.1 copy.31
  1.2 0.1 broadcast_compare_fusion
  1.3 0.8 constant_dynamic-slice_fusion
  2.2 0.1 copy.27
  2.2 0.1 copy.23
  2.3 0.1 copy.26
  2.4 6.9 %select_reduce_fusion.1 = (s32[8,8,9]{1,2,0:T(8,128)S(1)}, s32[8,8,9]{1,2,0:T(8,128)S(1)}, s32[8,8,9]{1,2,0:T(8,128)S(1)}, s32[8,8,9]{1,2,0:T(8,128)S(1)}, s32[8,8,9]{1,2,0:T(8,128)S(1)}) fusion(s32[8,16]{1,0:T(8,128)S(1)} %copy.26, s32[8,9]{1,0:T(8,128)S(1)} %get-tuple-element.25, s32[8,16]{1,0:T(8,128)S(1)} %iota_add_fusion.2, ...), kind=kLoop, calls=%fused_computation.1 | loop fusion | flops 181440 | bytes 14648 | tf_op jit(solution)/shard_map/reduce_max | solution.py:35
  9.3 0.3 copy.28
  9.6 0.1 reshape.145.table
  9.7 0.0 copy-start
  9.8 1.6 %copy-done = bf16[8,8,128,128]{3,2,1,0:T(8,128)(2,1)S(1)} copy-done((bf16[8,8,128,128]{3,2,1,0:T(8,128)(2,1)S(1)}, bf16[8,8,128,128]{3,2,1,0:T(8,128)(2,1)}, u32[]{:S(2)}) %copy-start) | copy-done | bytes 2097176
  11.3 79.4 %triangles.1 = f32[8,64]{1,0:T(8,128)S(1)} custom-call(s32[40,72]{1,0:T(8,128)S(1)} %reshape.145.table, bf16[8,8,128,128]{3,2,1,0:T(8,128)(2,1)S(1)} %copy-done), custom_call_target="tpu_custom_call" | custom-call | tf_op jit(solution)/shard_map/triangles/pallas_call | solution.py:263
  90.8 0.6 copy.37
  (9 shorter events, 0.1 us)
Async XLA Ops:
  9.7 1.6 %copy-start = (bf16[8,8,128,128]{3,2,1,0:T(8,128)(2,1)S(1)}, bf16[8,8,128,128]{3,2,1,0:T(8,128)(2,1)}, u32[]{:S(2)}) copy-start(bf16[8,8,128,128]{3,2,1,0:T(8,128)(2,1)} %tiles.1) | copy-start | bytes 6291460

commit v2 on v1

v2 whole, which is shorter than its diff:
```python
import functools

import jax
import jax.numpy as jnp
from jax import lax
from jax.experimental import pallas as pl
from jax.experimental.pallas import tpu as pltpu
from jax.sharding import PartitionSpec as P

MESH = pl.DeviceIdType.MESH
TILE = 128
ROWS = 8
HALF = 8
SLOTS = 16
NONE = ROWS * SLOTS
DIST = 4
PIECES = 4
PIECE = HALF // PIECES
PAIRS = ((0, 0), (0, -1), (0, -DIST), (1, -1), (-1, -DIST))
GROUPS = ((0, 3), (3, 3), (6, 1), (7, 1))


def group_of(c):
    return next(g for g, (first, size) in enumerate(GROUPS) if first <= c < first + size)


def kernel(
    blocks,
    cols_hbm,
    tiles,
    out,
    own,
    before,
    far,
    after_0,
    after_1,
    after_2,
    after_3,
    prior_0,
    prior_1,
    prior_2,
    prior_3,
    acc,
    given,
    got,
    cols,
    found,
    table,
    local_sem,
    keep_sem,
    cols_sem,
    table_sem,
    pair_send,
    pair_recv,
    far_send,
    far_recv,
    before_send,
    before_recv,
    after_send,
    after_recv,
    pass_before_send,
    pass_before_recv,
    pass_after_send,
    pass_after_recv,
    sum_send,
    sum_recv,
):
    after = (after_0, after_1, after_2, after_3)
    prior = (prior_0, prior_1, prior_2, prior_3)
    rep = lax.axis_index("rep")
    row = lax.axis_index("row")
    other = 1 - rep
    y = lax.rem(row, DIST)
    last_y = y == DIST - 1
    first_y = y == 0

    def at(step):
        return lax.rem(row + step + blocks, blocks)

    barrier = pltpu.get_barrier_semaphore()

    def greet(device):
        pl.semaphore_signal(barrier, inc=1, device_id=device, device_id_type=MESH)

    greet((other, row))
    for step in (1, -1):
        greet((rep, at(step)))
        greet((other, at(step)))
    for step in (DIST, -DIST):
        greet((rep, at(step)))

    @pl.when(last_y)
    def _():
        greet((rep, at(1 - DIST)))

    @pl.when(first_y)
    def _():
        greet((rep, at(DIST - 1)))

    def remote(source, target, send, recv, device):
        return pltpu.make_async_remote_copy(
            source, target, send, recv, device_id=device, device_id_type=MESH
        )

    def load(c):
        return pltpu.make_async_copy(
            tiles.at[c], own.at[pl.ds(c * SLOTS + rep * HALF, HALF)], local_sem.at[c]
        )

    def to_partner(c):
        return remote(
            tiles.at[c], own.at[pl.ds(c * SLOTS + rep * HALF, HALF)],
            pair_send.at[c], pair_recv.at[c], (other, row),
        )

    def to_far(c, h):
        piece = pl.ds(h * PIECE, PIECE)
        place = c * PIECES + h
        return remote(
            tiles.at[c, piece], far.at[c, piece],
            far_send.at[place], far_recv.at[place], (rep, at(DIST)),
        )

    def to_next(c, h):
        piece = pl.ds(h * PIECE, PIECE)
        place = c * PIECES + h
        return remote(
            tiles.at[c, piece], before.at[c, piece],
            before_send.at[place], before_recv.at[place], (rep, at(1)),
        )

    def relay(c, h):
        piece = pl.ds(h * PIECE, PIECE)
        place = c * PIECES + h
        return remote(
            far.at[c, piece], before.at[c, piece],
            before_send.at[place], before_recv.at[place], (rep, at(1 - DIST)),
        )

    def half_of(g, c):
        return pl.ds((c - GROUPS[g][0]) * SLOTS + rep * HALF, HALF)

    def to_previous(g, c):
        return remote(
            tiles.at[c], after[g].at[half_of(g, c)],
            after_send.at[c], after_recv.at[c], (rep, at(-1)),
        )

    def pass_after(g, c):
        return remote(
            after[g].at[half_of(g, c)], after[g].at[half_of(g, c)],
            pass_after_send.at[c], pass_after_recv.at[c], (other, row),
        )

    def pass_before(g, c):
        return remote(
            before.at[c], prior[g].at[half_of(g, c)],
            pass_before_send.at[c], pass_before_recv.at[c], (other, row),
        )

    def keep_before(g, c):
        return pltpu.make_async_copy(before.at[c], prior[g].at[half_of(g, c)], keep_sem.at[c])

    def per_group(c, action):
        for g, (first, size) in enumerate(GROUPS):

            @pl.when(jnp.logical_and(c >= first, c < first + size))
            def _():
                action(g)

    fetch = pltpu.make_async_copy(cols_hbm, cols, cols_sem)
    fetch.start()
    for c in range(ROWS):
        load(c).start()

    edge = jnp.logical_or(first_y, last_y).astype(jnp.int32)
    pl.semaphore_wait(barrier, 7 + edge)

    for c in range(ROWS):
        for h in range(PIECES):
            to_far(c, h).start()

            @pl.when(jnp.logical_not(last_y))
            def _():
                to_next(c, h).start()

        to_previous(group_of(c), c).start()
        to_partner(c).start()

    fetch.wait()
    known = cols[...].astype(jnp.float32)
    vertex = lax.broadcasted_iota(jnp.int32, (blocks * ROWS, TILE), 0)
    lane = lax.broadcasted_iota(jnp.int32, (blocks * ROWS, TILE), 1)

    def columns_at(wanted):
        pick = (vertex == wanted).astype(jnp.float32)
        return jnp.dot(
            known, pick, precision=lax.Precision.HIGHEST, preferred_element_type=jnp.float32
        ).astype(jnp.int32)

    of_k = {}
    for step in (0, -1, -DIST):
        both = columns_at(at(step) * ROWS + lane % ROWS)
        of_k[step] = jnp.where(rep == 0, both[:HALF], both[HALF:])
    of_i = {step: columns_at(at(step) * ROWS + lane // ROWS) for step in (0, 1, -1)}
    lane = lax.broadcasted_iota(jnp.int32, (HALF, TILE), 1)
    index_i = lane // ROWS
    first = jnp.zeros_like(lane)
    size = jnp.ones_like(lane)
    for begin, count in GROUPS:
        inside = index_i >= begin
        first = jnp.where(inside, begin, first)
        size = jnp.where(inside, count, size)
    for pair, (step_i, step_k) in enumerate(PAIRS):
        if step_i == 0:
            base, none = index_i * SLOTS, jnp.full_like(lane, NONE)
        else:
            base, none = (index_i - first) * SLOTS, size * SLOTS
        own_col = at(step_k) * ROWS + lane % ROWS
        for part, wanted in enumerate((of_k[step_k], own_col)):
            place = none
            for s in range(SLOTS):
                same = jnp.logical_and(wanted == of_i[step_i][s : s + 1], wanted >= 0)
                place = jnp.where(same, base + s, place)
            found[pair * SLOTS + part * HALF : pair * SLOTS + part * HALF + HALF] = place

    zero = jnp.zeros((TILE, TILE), jnp.bfloat16)
    own[NONE] = zero
    for g, (_, count) in enumerate(GROUPS):
        after[g][count * SLOTS] = zero
        prior[g][count * SLOTS] = zero
    acc[...] = jnp.zeros_like(acc)
    spread = pltpu.make_async_copy(found, table, table_sem)
    spread.start()

    @pl.loop(0, ROWS)
    def _(c):
        load(c).wait()
        to_partner(c).wait()

    spread.wait()

    def combine(pair, rows_i, tiles_k, total, c, members=range(ROWS)):
        right = jnp.concatenate(tiles_k, axis=1)
        for i in members:
            column = i * ROWS + c
            left = rows_i[table[pair * SLOTS + HALF, column]]
            product = jnp.dot(left, right, preferred_element_type=jnp.float32)
            here = acc[total * ROWS + i]
            for s in range(HALF):
                weight = rows_i[table[pair * SLOTS + s, column]]
                here += product[:, s * TILE : s * TILE + TILE] * weight.astype(jnp.float32)
            acc[total * ROWS + i] = here

    def row_of(ref, c):
        return [ref[c, s] for s in range(HALF)]

    def own_pairs(c):
        combine(2, own, row_of(far, c), 0, c)
        combine(1, own, row_of(before, c), 0, c)

    def away_pairs(g, c):
        members = range(GROUPS[g][0], GROUPS[g][0] + GROUPS[g][1])
        combine(3, after[g], row_of(before, c), 1, c, members)
        combine(4, prior[g], row_of(far, c), 2, c, members)

    def complete(g):
        for c in range(GROUPS[g][0], GROUPS[g][0] + GROUPS[g][1]):
            pass_after(g, c).wait_recv()
            pass_before(g, c).wait_recv()
            keep_before(g, c).wait()

    last = ROWS - 1

    @pl.loop(0, ROWS)
    def _(c):
        for h in range(PIECES):
            to_far(c, h).wait_recv()

            @pl.when(last_y)
            def _():
                relay(c, h).start()

        def on_after(g):
            to_previous(g, c).wait_recv()
            pass_after(g, c).start()

        per_group(c, on_after)
        for h in range(PIECES):
            to_next(c, h).wait_recv()

        def on_before(g):
            pass_before(g, c).start()
            keep_before(g, c).start()

        per_group(c, on_before)

        @pl.when(c < last)
        def _():
            @pl.loop(0, jnp.where(c == 3, 2, 1))
            def _(again):
                k = c + again * DIST
                combine(0, own, [own[k * SLOTS + rep * HALF + s] for s in range(HALF)], 0, k)

            own_pairs(c)

        for g in (0, 1):
            end = GROUPS[g][0] + GROUPS[g][1] - 1

            @pl.when(c == end)
            def _():
                complete(g)

            @pl.when(c >= end)
            def _():
                @pl.loop(jnp.where(c == end, 0, c), c + 1)
                def _(k):
                    away_pairs(g, k)

        @pl.when(c == last - 1)
        def _():
            complete(2)

        @pl.when(c >= last - 1)
        def _():
            late = c - (last - 1)

            @pl.loop(late * 3, 3 + late)
            def _(k):
                away_pairs(2, 2 * k)
                away_pairs(2, 2 * k + 1)

    complete(3)

    @pl.loop(0, ROWS // 2)
    def _(k):
        away_pairs(3, 2 * k)
        away_pairs(3, 2 * k + 1)

    def sum_copy(slot, source, device):
        return remote(given.at[source], got.at[slot], sum_send.at[slot], sum_recv.at[slot], device)

    def add_up(t):
        given[t] = jnp.sum(acc[t * ROWS : t * ROWS + ROWS], axis=-1)

    sums = [
        sum_copy(1, 1, (rep, at(1))),
        sum_copy(2, 1, (other, at(1))),
        sum_copy(3, 2, (rep, at(-1))),
        sum_copy(4, 2, (other, at(-1))),
    ]
    add_up(1)
    add_up(2)
    for copy in sums:
        copy.start()
    own_pairs(last)
    add_up(0)
    sums.append(sum_copy(0, 0, (other, row)))
    sums[-1].start()
    for copy in sums:
        copy.wait()
    total = given[0]
    for slot in range(5):
        total += got[slot]
    out[...] = jnp.where(rep == 0, total[:, : TILE // 2], total[:, TILE // 2 :])

    for c in range(ROWS):
        for h in range(PIECES):
            to_far(c, h).wait_send()
            to_next(c, h).wait_send()
        g = group_of(c)
        to_previous(g, c).wait_send()
        pass_after(g, c).wait_send()
        pass_before(g, c).wait_send()


def body(blocks, tiles, tile_cols):
    dma = pltpu.SemaphoreType.DMA

    def stack(count):
        return pltpu.VMEM((count, TILE, TILE), jnp.bfloat16)

    half = pltpu.VMEM((ROWS, HALF, TILE, TILE), jnp.bfloat16)
    groups = [stack(count * SLOTS + 1) for _, count in GROUPS]
    pieces = ROWS * PIECES
    return pl.pallas_call(
        functools.partial(kernel, blocks),
        out_shape=jax.ShapeDtypeStruct((ROWS, TILE // 2), jnp.float32),
        in_specs=[
            pl.BlockSpec(memory_space=pltpu.HBM),
            pl.BlockSpec(memory_space=pltpu.HBM),
        ],
        out_specs=pl.BlockSpec(memory_space=pltpu.VMEM),
        scratch_shapes=[
            stack(NONE + 1),
            half,
            half,
            *groups,
            *groups,
            pltpu.VMEM((3 * ROWS, TILE, TILE), jnp.float32),
            pltpu.VMEM((3, ROWS, TILE), jnp.float32),
            pltpu.VMEM((5, ROWS, TILE), jnp.float32),
            pltpu.VMEM((SLOTS, blocks * ROWS), jnp.int32),
            pltpu.VMEM((len(PAIRS) * SLOTS, TILE), jnp.int32),
            pltpu.SMEM((len(PAIRS) * SLOTS, TILE), jnp.int32),
            dma((ROWS,)),
            dma((ROWS,)),
            dma,
            dma,
            dma((ROWS,)),
            dma((ROWS,)),
            dma((pieces,)),
            dma((pieces,)),
            dma((pieces,)),
            dma((pieces,)),
            dma((ROWS,)),
            dma((ROWS,)),
            dma((ROWS,)),
            dma((ROWS,)),
            dma((ROWS,)),
            dma((ROWS,)),
            dma((5,)),
            dma((5,)),
        ],
        compiler_params=pltpu.CompilerParams(
            collective_id=0, has_side_effects=True, vmem_limit_bytes=67_030_000
        ),
        name="triangles",
    )(tile_cols.T, tiles)


def solution(mesh):
    return jax.shard_map(
        functools.partial(body, mesh.shape["row"]),
        mesh=mesh,
        in_specs=(P("row", "rep", None, None), P()),
        out_specs=P("row", "rep"),
        check_vma=False,
    )
```

time: 91.6 us -> 74.6 us (0.81)
  other arithmetic: 7.15 us -> 0 us
  Pallas kernels: 79.4 us -> 72.9 us
  local copies, waits for them, and re-layouts: 4.71 us -> 1.28 us
    reduce_max x1 -> x0, other arithmetic: 6.86 us -> none  [lookup_table(): found = jnp.max(jnp.where(same, place[None, :, None, :], -1), axis=-1)]
    pallas_call x1, Pallas kernels: 79.4 us -> 72.9 us  [body(): pl.pallas_call(functools.partial(kernel, blocks), out_shape=jax.ShapeDtyp...]
    dynamic_slice x5 -> x0, local copies, waits for them, and re-layouts: 1.91 us -> none  [the longest x4 1.05 us: lookup_table(): lax.dynamic_slice_in_dim(tile_cols, lax.rem(row + d + blocks, blocks) * R...]
    unnamed x6 -> x1, local copies, waits for them, and re-layouts: 2.39 us -> 1.28 us
where the time goes in v2:
time: 74.6 us; the launch traced here: 74.2 us
  Pallas kernels  72.9 us (98%)
  local copies, waits for them, and re-layouts  1.28 us (2%)
    pallas_call x1, Pallas kernels, body(): pl.pallas_call(functools.partial(kernel, blocks), out_shape=jax.ShapeDtyp...  72.9 us

profile of v2, /device:TPU:1, one launch (start us, length us, event | category | flops | bytes accessed | tf_op | source)
XLA Modules:
  0.0 74.2 jit_solution(8563124606235729731)
XLA Ops:
  0.0 72.9 %triangles.1 = f32[8,64]{1,0:T(8,128)} custom-call(s32[16,512]{1,0:T(8,128)} %bitcast.1, bf16[8,8,128,128]{3,2,1,0:T(8,128)(2,1)} %tiles.1), custom_call_target="tpu_custom_call" | custom-call | tf_op jit(solution)/shard_map/triangles/pallas_call | solution.py:386
  72.9 1.3 %copy.4 = f32[8,64]{1,0:T(8,128)} copy(f32[8,64]{1,0:T(8,128)} %triangles.1) | data formatting | bytes 4096

commit v3 on v2

--- a/solution.py
+++ b/solution.py
@@ -44,6 +44,8 @@
     given,
     got,
     cols,
+    of_k,
+    of_i,
     found,
     table,
     local_sem,
@@ -187,6 +189,13 @@
         to_previous(group_of(c), c).start()
         to_partner(c).start()
 
+    def relay_piece(c, h):
+        to_far(c, h).wait_recv()
+
+        @pl.when(last_y)
+        def _():
+            relay(c, h).start()
+
     fetch.wait()
     known = cols[...].astype(jnp.float32)
     vertex = lax.broadcasted_iota(jnp.int32, (blocks * ROWS, TILE), 0)
@@ -198,11 +207,13 @@
             known, pick, precision=lax.Precision.HIGHEST, preferred_element_type=jnp.float32
         ).astype(jnp.int32)
 
-    of_k = {}
-    for step in (0, -1, -DIST):
+    for t, step in enumerate((0, -1, -DIST)):
         both = columns_at(at(step) * ROWS + lane % ROWS)
-        of_k[step] = jnp.where(rep == 0, both[:HALF], both[HALF:])
-    of_i = {step: columns_at(at(step) * ROWS + lane // ROWS) for step in (0, 1, -1)}
+        of_k[t] = jnp.where(rep == 0, both[:HALF], both[HALF:])
+    relay_piece(0, 0)
+    for t, step in enumerate((0, 1, -1)):
+        of_i[t] = columns_at(at(step) * ROWS + lane // ROWS)
+    relay_piece(0, 1)
     lane = lax.broadcasted_iota(jnp.int32, (HALF, TILE), 1)
     index_i = lane // ROWS
     first = jnp.zeros_like(lane)
@@ -217,13 +228,15 @@
         else:
             base, none = (index_i - first) * SLOTS, size * SLOTS
         own_col = at(step_k) * ROWS + lane % ROWS
-        for part, wanted in enumerate((of_k[step_k], own_col)):
+        named = of_k[(0, -1, -DIST).index(step_k)]
+        held = of_i[(0, 1, -1).index(step_i)]
+        for part, wanted in enumerate((named, own_col)):
             place = none
             for s in range(SLOTS):
-                same = jnp.logical_and(wanted == of_i[step_i][s : s + 1], wanted >= 0)
+                same = jnp.logical_and(wanted == held[s : s + 1], wanted >= 0)
                 place = jnp.where(same, base + s, place)
             found[pair * SLOTS + part * HALF : pair * SLOTS + part * HALF + HALF] = place
-
+    relay_piece(0, 2)
     zero = jnp.zeros((TILE, TILE), jnp.bfloat16)
     own[NONE] = zero
     for g, (_, count) in enumerate(GROUPS):
@@ -232,13 +245,7 @@
     acc[...] = jnp.zeros_like(acc)
     spread = pltpu.make_async_copy(found, table, table_sem)
     spread.start()
-
-    @pl.loop(0, ROWS)
-    def _(c):
-        load(c).wait()
-        to_partner(c).wait()
-
-    spread.wait()
+    relay_piece(0, 3)
 
     def combine(pair, rows_i, tiles_k, total, c, members=range(ROWS)):
         right = jnp.concatenate(tiles_k, axis=1)
@@ -272,15 +279,7 @@
 
     last = ROWS - 1
 
-    @pl.loop(0, ROWS)
-    def _(c):
-        for h in range(PIECES):
-            to_far(c, h).wait_recv()
-
-            @pl.when(last_y)
-            def _():
-                relay(c, h).start()
-
+    def arrivals(c):
         def on_after(g):
             to_previous(g, c).wait_recv()
             pass_after(g, c).start()
@@ -295,41 +294,91 @@
 
         per_group(c, on_before)
 
-        @pl.when(c < last)
-        def _():
-            @pl.loop(0, jnp.where(c == 3, 2, 1))
-            def _(again):
-                k = c + again * DIST
-                combine(0, own, [own[k * SLOTS + rep * HALF + s] for s in range(HALF)], 0, k)
-
-            own_pairs(c)
-
-        for g in (0, 1):
-            end = GROUPS[g][0] + GROUPS[g][1] - 1
-
-            @pl.when(c == end)
-            def _():
-                complete(g)
-
-            @pl.when(c >= end)
-            def _():
-                @pl.loop(jnp.where(c == end, 0, c), c + 1)
-                def _(k):
-                    away_pairs(g, k)
-
-        @pl.when(c == last - 1)
+    def spans(p, *entries):
+        begin, end = 0, 0
+        for when, low, high in entries:
+            begin = jnp.where(when, low, begin)
+            end = jnp.where(when, high, end)
+        return begin, end
+
+    @pl.loop(PIECES, ROWS * PIECES)
+    def _(p):
+        c = p // PIECES
+        h = lax.rem(p, PIECES)
+        relay_piece(c, h)
+
+        @pl.when(h == 0)
+        def _():
+            arrivals(c - 1)
+
+        @pl.when(p == 2 * PIECES)
+        def _():
+            @pl.loop(0, ROWS)
+            def _(k):
+                load(k).wait()
+                to_partner(k).wait()
+
+            spread.wait()
+
+        def both(*tests):
+            return functools.reduce(jnp.logical_and, tests)
+
+        begin, end = spans(
+            p,
+            (both(h == 0, c >= 2), c - 1, c),
+            (p == 11, 0, 1),
+        )
+
+        @pl.loop(begin, end)
+        def _(k):
+            own_pairs(k)
+
+        begin, end = spans(p, (both(h == 1, c >= 2, c <= 5), 2 * c - 4, 2 * c - 2))
+
+        @pl.loop(begin, end)
+        def _(k):
+            combine(0, own, [own[k * SLOTS + rep * HALF + s] for s in range(HALF)], 0, k)
+
+        @pl.when(p == 14)
+        def _():
+            complete(0)
+
+        begin, end = spans(
+            p, (both(h == 2, c >= 4), c - 1, c), (p == 14, 0, 2), (p == 15, 2, 3)
+        )
+
+        @pl.loop(begin, end)
+        def _(k):
+            away_pairs(0, k)
+
+        @pl.when(p == 25)
+        def _():
+            complete(1)
+
+        begin, end = spans(
+            p, (p == 25, 0, 2), (p == 26, 2, 4), (p == 27, 4, 6), (p == 30, 6, 7)
+        )
+
+        @pl.loop(begin, end)
+        def _(k):
+            away_pairs(1, k)
+
+        @pl.when(p == 29)
         def _():
             complete(2)
 
-        @pl.when(c >= last - 1)
-        def _():
-            late = c - (last - 1)
-
-            @pl.loop(late * 3, 3 + late)
-            def _(k):
-                away_pairs(2, 2 * k)
-                away_pairs(2, 2 * k + 1)
-
+        begin, end = spans(p, (p == 29, 0, 2), (p == 31, 2, 3))
+
+        @pl.loop(begin, end)
+        def _(k):
+            away_pairs(2, 2 * k)
+            away_pairs(2, 2 * k + 1)
+
+    arrivals(last)
+    away_pairs(0, last)
+    away_pairs(1, last)
+    away_pairs(2, last - 1)
+    away_pairs(2, last)
     complete(3)
 
     @pl.loop(0, ROWS // 2)
@@ -401,6 +450,8 @@
             pltpu.VMEM((3, ROWS, TILE), jnp.float32),
             pltpu.VMEM((5, ROWS, TILE), jnp.float32),
             pltpu.VMEM((SLOTS, blocks * ROWS), jnp.int32),
+            pltpu.VMEM((3, HALF, TILE), jnp.int32),
+            pltpu.VMEM((3, SLOTS, TILE), jnp.int32),
             pltpu.VMEM((len(PAIRS) * SLOTS, TILE), jnp.int32),
             pltpu.SMEM((len(PAIRS) * SLOTS, TILE), jnp.int32),
             dma((ROWS,)),

time: 74.6 us -> 72.6 us (0.973)
  Pallas kernels: 72.9 us -> 71.1 us
    pallas_call x1, Pallas kernels: 72.9 us -> 71.1 us  [body(): pl.pallas_call(functools.partial(kernel, blocks), out_shape=jax.ShapeDtyp...]
where the time goes in v3:
time: 72.6 us; the launch traced here: 72.4 us
  Pallas kernels  71.1 us (98%)
  local copies, waits for them, and re-layouts  1.28 us (2%)
    pallas_call x1, Pallas kernels, body(): pl.pallas_call(functools.partial(kernel, blocks), out_shape=jax.ShapeDtyp...  71.1 us

profile of v3, /device:TPU:1, one launch (start us, length us, event | category | flops | bytes accessed | tf_op | source)
XLA Modules:
  0.0 72.4 jit_solution(13417268851284526270)
XLA Ops:
  0.0 71.1 %triangles.1 = f32[8,64]{1,0:T(8,128)} custom-call(s32[16,512]{1,0:T(8,128)} %bitcast.1, bf16[8,8,128,128]{3,2,1,0:T(8,128)(2,1)} %tiles.1), custom_call_target="tpu_custom_call" | custom-call | tf_op jit(solution)/shard_map/triangles/pallas_call | solution.py:435
  71.2 1.3 %copy.4 = f32[8,64]{1,0:T(8,128)} copy(f32[8,64]{1,0:T(8,128)} %triangles.1) | data formatting | bytes 4096

commit v4 on v3

--- a/solution.py
+++ b/solution.py
@@ -52,6 +52,7 @@
     keep_sem,
     cols_sem,
     table_sem,
+    fill_sem,
     pair_send,
     pair_recv,
     far_send,
@@ -66,6 +67,7 @@
     pass_after_recv,
     sum_send,
     sum_recv,
+    relay_send,
 ):
     after = (after_0, after_1, after_2, after_3)
     prior = (prior_0, prior_1, prior_2, prior_3)
@@ -75,6 +77,11 @@
     y = lax.rem(row, DIST)
     last_y = y == DIST - 1
     first_y = y == 0
+    top = row == blocks - 1
+    has_far = jnp.logical_or(row >= DIST, row == 0)
+    gives_far = row <= blocks - DIST
+    relays = jnp.logical_and(last_y, row >= DIST)
+    gives_next = jnp.logical_or(jnp.logical_not(last_y), top)
 
     def at(step):
         return lax.rem(row + step + blocks, blocks)
@@ -136,7 +143,7 @@
         place = c * PIECES + h
         return remote(
             far.at[c, piece], before.at[c, piece],
-            before_send.at[place], before_recv.at[place], (rep, at(1 - DIST)),
+            relay_send.at[place], before_recv.at[place], (rep, at(1 - DIST)),
         )
 
     def half_of(g, c):
@@ -178,11 +185,20 @@
     edge = jnp.logical_or(first_y, last_y).astype(jnp.int32)
     pl.semaphore_wait(barrier, 7 + edge)
 
+    fill = pltpu.make_async_copy(tiles, far, fill_sem)
+
+    @pl.when(jnp.logical_not(has_far))
+    def _():
+        fill.start()
+
     for c in range(ROWS):
         for h in range(PIECES):
-            to_far(c, h).start()
-
-            @pl.when(jnp.logical_not(last_y))
+
+            @pl.when(gives_far)
+            def _():
+                to_far(c, h).start()
+
+            @pl.when(gives_next)
             def _():
                 to_next(c, h).start()
 
@@ -190,9 +206,11 @@
         to_partner(c).start()
 
     def relay_piece(c, h):
-        to_far(c, h).wait_recv()
-
-        @pl.when(last_y)
+        @pl.when(has_far)
+        def _():
+            to_far(c, h).wait_recv()
+
+        @pl.when(relays)
         def _():
             relay(c, h).start()
 
@@ -320,6 +338,10 @@
 
             spread.wait()
 
+            @pl.when(jnp.logical_not(has_far))
+            def _():
+                fill.wait()
+
         def both(*tests):
             return functools.reduce(jnp.logical_and, tests)
 
@@ -392,22 +414,35 @@
     def add_up(t):
         given[t] = jnp.sum(acc[t * ROWS : t * ROWS + ROWS], axis=-1)
 
-    sums = [
-        sum_copy(1, 1, (rep, at(1))),
-        sum_copy(2, 1, (other, at(1))),
-        sum_copy(3, 2, (rep, at(-1))),
-        sum_copy(4, 2, (other, at(-1))),
-    ]
+    up = [sum_copy(1, 1, (rep, at(1))), sum_copy(2, 1, (other, at(1)))]
+    down = [sum_copy(3, 2, (rep, at(-1))), sum_copy(4, 2, (other, at(-1)))]
+    across = sum_copy(0, 0, (other, row))
     add_up(1)
     add_up(2)
-    for copy in sums:
+
+    @pl.when(jnp.logical_not(top))
+    def _():
+        for copy in up:
+            copy.start()
+
+    for copy in down:
         copy.start()
     own_pairs(last)
     add_up(0)
-    sums.append(sum_copy(0, 0, (other, row)))
-    sums[-1].start()
-    for copy in sums:
+    across.start()
+
+    @pl.when(row == 0)
+    def _():
+        got[1:3] = jnp.zeros((2, ROWS, TILE), jnp.float32)
+
+    @pl.when(row > 0)
+    def _():
+        for copy in up:
+            copy.wait_recv()
+
+    for copy in down:
         copy.wait()
+    across.wait()
     total = given[0]
     for slot in range(5):
         total += got[slot]
@@ -415,12 +450,27 @@
 
     for c in range(ROWS):
         for h in range(PIECES):
-            to_far(c, h).wait_send()
-            to_next(c, h).wait_send()
+            @pl.when(gives_far)
+            def _():
+                to_far(c, h).wait_send()
+
+            @pl.when(gives_next)
+            def _():
+                to_next(c, h).wait_send()
+
+            @pl.when(relays)
+            def _():
+                relay(c, h).wait_send()
+
         g = group_of(c)
         to_previous(g, c).wait_send()
         pass_after(g, c).wait_send()
         pass_before(g, c).wait_send()
+
+    @pl.when(jnp.logical_not(top))
+    def _():
+        for copy in up:
+            copy.wait_send()
 
 
 def body(blocks, tiles, tile_cols):
@@ -458,6 +508,7 @@
             dma((ROWS,)),
             dma,
             dma,
+            dma,
             dma((ROWS,)),
             dma((ROWS,)),
             dma((pieces,)),
@@ -472,6 +523,7 @@
             dma((ROWS,)),
             dma((5,)),
             dma((5,)),
+            dma((pieces,)),
         ],
         compiler_params=pltpu.CompilerParams(
             collective_id=0, has_side_effects=True, vmem_limit_bytes=67_030_000

time: 72.6 us -> 113 us (1.56)
  Pallas kernels: 71.1 us -> 111 us
    pallas_call x1, Pallas kernels: 71.1 us -> 111 us  [body(): pl.pallas_call(functools.partial(kernel, blocks), out_shape=jax.ShapeDtyp...]
where the time goes in v4:
time: 113 us
  Pallas kernels  111 us (98%)
  local copies, waits for them, and re-layouts  1.28 us (1%)
    pallas_call x1, Pallas kernels, body(): pl.pallas_call(functools.partial(kernel, blocks), out_shape=jax.ShapeDtyp...  111 us

profile of v4, /device:TPU:1, one launch (start us, length us, event | category | flops | bytes accessed | tf_op | source)
XLA Modules:
  0.0 112.7 jit_solution(163136256320124373)
XLA Ops:
  0.0 111.4 %triangles.1 = f32[8,64]{1,0:T(8,128)} custom-call(s32[16,512]{1,0:T(8,128)} %bitcast.1, bf16[8,8,128,128]{3,2,1,0:T(8,128)(2,1)} %tiles.1), custom_call_target="tpu_custom_call" | custom-call | tf_op jit(solution)/shard_map/triangles/pallas_call | solution.py:485
  111.4 1.3 %copy.4 = f32[8,64]{1,0:T(8,128)} copy(f32[8,64]{1,0:T(8,128)} %triangles.1) | data formatting | bytes 4096

commit v5 on v4

--- a/solution.py
+++ b/solution.py
@@ -78,10 +78,9 @@
     last_y = y == DIST - 1
     first_y = y == 0
     top = row == blocks - 1
-    has_far = jnp.logical_or(row >= DIST, row == 0)
-    gives_far = row <= blocks - DIST
-    relays = jnp.logical_and(last_y, row >= DIST)
-    gives_next = jnp.logical_or(jnp.logical_not(last_y), top)
+    has_far = jnp.logical_or(row >= DIST - 1, row == 0)
+    gives_far = jnp.logical_or(row <= blocks - DIST, top)
+    gives_next = jnp.logical_not(last_y)
 
     def at(step):
         return lax.rem(row + step + blocks, blocks)
@@ -210,7 +209,7 @@
         def _():
             to_far(c, h).wait_recv()
 
-        @pl.when(relays)
+        @pl.when(last_y)
         def _():
             relay(c, h).start()
 
@@ -458,7 +457,7 @@
             def _():
                 to_next(c, h).wait_send()
 
-            @pl.when(relays)
+            @pl.when(last_y)
             def _():
                 relay(c, h).wait_send()
 

time: 113 us -> 70.9 us (0.63)
  Pallas kernels: 111 us -> 69.5 us
    pallas_call x1, Pallas kernels: 111 us -> 69.5 us  [body(): pl.pallas_call(functools.partial(kernel, blocks), out_shape=jax.ShapeDtyp...]
where the time goes in v5:
time: 70.9 us; the launch traced here: 70.7 us
  Pallas kernels  69.5 us (98%)
  local copies, waits for them, and re-layouts  1.28 us (2%)
    pallas_call x1, Pallas kernels, body(): pl.pallas_call(functools.partial(kernel, blocks), out_shape=jax.ShapeDtyp...  69.5 us

profile of v5, /device:TPU:1, one launch (start us, length us, event | category | flops | bytes accessed | tf_op | source)
XLA Modules:
  0.0 70.7 jit_solution(13376343094121545801)
XLA Ops:
  0.0 69.5 %triangles.1 = f32[8,64]{1,0:T(8,128)} custom-call(s32[16,512]{1,0:T(8,128)} %bitcast.1, bf16[8,8,128,128]{3,2,1,0:T(8,128)(2,1)} %tiles.1), custom_call_target="tpu_custom_call" | custom-call | tf_op jit(solution)/shard_map/triangles/pallas_call | solution.py:484
  69.5 1.3 %copy.4 = f32[8,64]{1,0:T(8,128)} copy(f32[8,64]{1,0:T(8,128)} %triangles.1) | data formatting | bytes 4096

commit v6 on v5

--- a/solution.py
+++ b/solution.py
@@ -53,6 +53,7 @@
     cols_sem,
     table_sem,
     fill_sem,
+    stand_sem,
     pair_send,
     pair_recv,
     far_send,
@@ -91,15 +92,15 @@
         pl.semaphore_signal(barrier, inc=1, device_id=device, device_id_type=MESH)
 
     greet((other, row))
-    for step in (1, -1):
-        greet((rep, at(step)))
-        greet((other, at(step)))
-    for step in (DIST, -DIST):
-        greet((rep, at(step)))
-
-    @pl.when(last_y)
-    def _():
-        greet((rep, at(1 - DIST)))
+    greet((rep, at(-DIST)))
+
+    @pl.when(row > 0)
+    def _():
+        greet((rep, at(-1)))
+
+    @pl.when(jnp.logical_not(top))
+    def _():
+        greet((rep, at(1)))
 
     @pl.when(first_y)
     def _():
@@ -168,6 +169,9 @@
 
     def keep_before(g, c):
         return pltpu.make_async_copy(before.at[c], prior[g].at[half_of(g, c)], keep_sem.at[c])
+
+    def stand_in(g, c):
+        return pltpu.make_async_copy(tiles.at[c], after[g].at[half_of(g, c)], stand_sem.at[c])
 
     def per_group(c, action):
         for g, (first, size) in enumerate(GROUPS):
@@ -181,8 +185,8 @@
     for c in range(ROWS):
         load(c).start()
 
-    edge = jnp.logical_or(first_y, last_y).astype(jnp.int32)
-    pl.semaphore_wait(barrier, 7 + edge)
+    ends = jnp.logical_or(row == 0, top).astype(jnp.int32)
+    pl.semaphore_wait(barrier, 4 - ends + last_y.astype(jnp.int32))
 
     fill = pltpu.make_async_copy(tiles, far, fill_sem)
 
@@ -201,7 +205,14 @@
             def _():
                 to_next(c, h).start()
 
-        to_previous(group_of(c), c).start()
+        @pl.when(row > 0)
+        def _():
+            to_previous(group_of(c), c).start()
+
+        @pl.when(top)
+        def _():
+            stand_in(group_of(c), c).start()
+
         to_partner(c).start()
 
     def relay_piece(c, h):
@@ -283,25 +294,49 @@
         combine(2, own, row_of(far, c), 0, c)
         combine(1, own, row_of(before, c), 0, c)
 
+    def up_pair(g, c):
+        combine(3, after[g], row_of(before, c), 1, c, rows_in(g))
+
+    def down_pair(g, c):
+        combine(4, prior[g], row_of(far, c), 2, c, rows_in(g))
+
     def away_pairs(g, c):
-        members = range(GROUPS[g][0], GROUPS[g][0] + GROUPS[g][1])
-        combine(3, after[g], row_of(before, c), 1, c, members)
-        combine(4, prior[g], row_of(far, c), 2, c, members)
-
-    def complete(g):
-        for c in range(GROUPS[g][0], GROUPS[g][0] + GROUPS[g][1]):
+        up_pair(g, c)
+        down_pair(g, c)
+
+    def rows_in(g):
+        return range(GROUPS[g][0], GROUPS[g][0] + GROUPS[g][1])
+
+    def complete_after(g):
+        for c in rows_in(g):
             pass_after(g, c).wait_recv()
+
+    def complete_prior(g):
+        for c in rows_in(g):
             pass_before(g, c).wait_recv()
             keep_before(g, c).wait()
 
+    def complete(g):
+        complete_after(g)
+        complete_prior(g)
+
     last = ROWS - 1
 
-    def arrivals(c):
+    def after_arrives(c):
         def on_after(g):
-            to_previous(g, c).wait_recv()
+            @pl.when(jnp.logical_not(top))
+            def _():
+                to_previous(g, c).wait_recv()
+
+            @pl.when(top)
+            def _():
+                stand_in(g, c).wait()
+
             pass_after(g, c).start()
 
         per_group(c, on_after)
+
+    def before_arrives(c):
         for h in range(PIECES):
             to_next(c, h).wait_recv()
 
@@ -310,6 +345,10 @@
             keep_before(g, c).start()
 
         per_group(c, on_before)
+
+    def arrivals(c):
+        after_arrives(c)
+        before_arrives(c)
 
     def spans(p, *entries):
         begin, end = 0, 0
@@ -395,17 +434,22 @@
             away_pairs(2, 2 * k)
             away_pairs(2, 2 * k + 1)
 
-    arrivals(last)
-    away_pairs(0, last)
-    away_pairs(1, last)
+    after_arrives(last)
     away_pairs(2, last - 1)
-    away_pairs(2, last)
-    complete(3)
-
-    @pl.loop(0, ROWS // 2)
+    for g in range(3):
+        down_pair(g, last)
+    complete_after(3)
+
+    @pl.loop(0, 3)
     def _(k):
-        away_pairs(3, 2 * k)
-        away_pairs(3, 2 * k + 1)
+        up_pair(3, 2 * k)
+        up_pair(3, 2 * k + 1)
+
+    up_pair(3, last - 1)
+    combine(2, own, row_of(far, last), 0, last)
+    before_arrives(last)
+    for g in range(4):
+        up_pair(g, last)
 
     def sum_copy(slot, source, device):
         return remote(given.at[source], got.at[slot], sum_send.at[slot], sum_recv.at[slot], device)
@@ -417,16 +461,23 @@
     down = [sum_copy(3, 2, (rep, at(-1))), sum_copy(4, 2, (other, at(-1)))]
     across = sum_copy(0, 0, (other, row))
     add_up(1)
-    add_up(2)
 
     @pl.when(jnp.logical_not(top))
     def _():
         for copy in up:
             copy.start()
 
+    combine(1, own, row_of(before, last), 0, last)
+    complete_prior(3)
+
+    @pl.loop(0, ROWS // 4)
+    def _(k):
+        for j in range(4):
+            down_pair(3, 4 * k + j)
+
+    add_up(2)
     for copy in down:
         copy.start()
-    own_pairs(last)
     add_up(0)
     across.start()
 
@@ -462,7 +513,11 @@
                 relay(c, h).wait_send()
 
         g = group_of(c)
-        to_previous(g, c).wait_send()
+
+        @pl.when(row > 0)
+        def _():
+            to_previous(g, c).wait_send()
+
         pass_after(g, c).wait_send()
         pass_before(g, c).wait_send()
 
@@ -510,6 +565,7 @@
             dma,
             dma((ROWS,)),
             dma((ROWS,)),
+            dma((ROWS,)),
             dma((pieces,)),
             dma((pieces,)),
             dma((pieces,)),

time: 70.9 us -> 70.9 us (level)
  no operation moved by 1% of the time
where the time goes in v6:
time: 70.9 us; the launch traced here: 70.8 us
  Pallas kernels  69.5 us (98%)
  local copies, waits for them, and re-layouts  1.28 us (2%)
    pallas_call x1, Pallas kernels, body(): pl.pallas_call(functools.partial(kernel, blocks), out_shape=jax.ShapeDtyp...  69.5 us

profile of v6, /device:TPU:1, one launch (start us, length us, event | category | flops | bytes accessed | tf_op | source)
XLA Modules:
  0.0 70.8 jit_solution(4672320985190036985)
XLA Ops:
  0.0 69.5 %triangles.1 = f32[8,64]{1,0:T(8,128)} custom-call(s32[16,512]{1,0:T(8,128)} %bitcast.1, bf16[8,8,128,128]{3,2,1,0:T(8,128)(2,1)} %tiles.1), custom_call_target="tpu_custom_call" | custom-call | tf_op jit(solution)/shard_map/triangles/pallas_call | solution.py:539
  69.5 1.3 %copy.4 = f32[8,64]{1,0:T(8,128)} copy(f32[8,64]{1,0:T(8,128)} %triangles.1) | data formatting | bytes 4096

commit v7 on v6

--- a/solution.py
+++ b/solution.py
@@ -146,6 +146,19 @@
             relay_send.at[place], before_recv.at[place], (rep, at(1 - DIST)),
         )
 
+    def far_row(c):
+        place = c * PIECES
+        return remote(
+            tiles.at[c], far.at[c], far_send.at[place], far_recv.at[place], (rep, at(DIST))
+        )
+
+    def next_row(c):
+        place = c * PIECES
+        return remote(
+            tiles.at[c], before.at[c],
+            before_send.at[place], before_recv.at[place], (rep, at(1)),
+        )
+
     def half_of(g, c):
         return pl.ds((c - GROUPS[g][0]) * SLOTS + rep * HALF, HALF)
 
@@ -195,15 +208,18 @@
         fill.start()
 
     for c in range(ROWS):
-        for h in range(PIECES):
-
-            @pl.when(gives_far)
-            def _():
+        @pl.when(jnp.logical_and(gives_far, last_y))
+        def _():
+            for h in range(PIECES):
                 to_far(c, h).start()
 
-            @pl.when(gives_next)
-            def _():
-                to_next(c, h).start()
+        @pl.when(jnp.logical_and(gives_far, jnp.logical_not(last_y)))
+        def _():
+            far_row(c).start()
+
+        @pl.when(gives_next)
+        def _():
+            next_row(c).start()
 
         @pl.when(row > 0)
         def _():
@@ -216,13 +232,18 @@
         to_partner(c).start()
 
     def relay_piece(c, h):
-        @pl.when(has_far)
+        @pl.when(last_y)
         def _():
             to_far(c, h).wait_recv()
-
-        @pl.when(last_y)
-        def _():
             relay(c, h).start()
+
+        @pl.when(
+            functools.reduce(
+                jnp.logical_and, (has_far, jnp.logical_not(last_y), h == PIECES - 1)
+            )
+        )
+        def _():
+            far_row(c).wait_recv()
 
     fetch.wait()
     known = cols[...].astype(jnp.float32)
@@ -337,8 +358,14 @@
         per_group(c, on_after)
 
     def before_arrives(c):
-        for h in range(PIECES):
-            to_next(c, h).wait_recv()
+        @pl.when(first_y)
+        def _():
+            for h in range(PIECES):
+                to_next(c, h).wait_recv()
+
+        @pl.when(jnp.logical_not(first_y))
+        def _():
+            next_row(c).wait_recv()
 
         def on_before(g):
             pass_before(g, c).start()
@@ -447,9 +474,6 @@
 
     up_pair(3, last - 1)
     combine(2, own, row_of(far, last), 0, last)
-    before_arrives(last)
-    for g in range(4):
-        up_pair(g, last)
 
     def sum_copy(slot, source, device):
         return remote(given.at[source], got.at[slot], sum_send.at[slot], sum_recv.at[slot], device)
@@ -460,26 +484,46 @@
     up = [sum_copy(1, 1, (rep, at(1))), sum_copy(2, 1, (other, at(1)))]
     down = [sum_copy(3, 2, (rep, at(-1))), sum_copy(4, 2, (other, at(-1)))]
     across = sum_copy(0, 0, (other, row))
-    add_up(1)
-
-    @pl.when(jnp.logical_not(top))
+    @pl.when(row == 0)
+    def _():
+        add_up(0)
+        add_up(1)
+        for copy in (across, *up):
+            copy.start()
+
+    before_arrives(last)
+
+    @pl.when(row > 0)
+    def _():
+        for g in range(4):
+            up_pair(g, last)
+
+    @pl.when(row > 0)
+    def _():
+        add_up(1)
+
+    @pl.when(jnp.logical_and(row > 0, jnp.logical_not(top)))
     def _():
         for copy in up:
             copy.start()
 
-    combine(1, own, row_of(before, last), 0, last)
     complete_prior(3)
 
-    @pl.loop(0, ROWS // 4)
-    def _(k):
-        for j in range(4):
-            down_pair(3, 4 * k + j)
+    for k in range(ROWS):
+        down_pair(3, k)
 
     add_up(2)
     for copy in down:
         copy.start()
-    add_up(0)
-    across.start()
+
+    @pl.when(row > 0)
+    def _():
+        combine(1, own, row_of(before, last), 0, last)
+
+    @pl.when(row > 0)
+    def _():
+        add_up(0)
+        across.start()
 
     @pl.when(row == 0)
     def _():
@@ -499,17 +543,22 @@
     out[...] = jnp.where(rep == 0, total[:, : TILE // 2], total[:, TILE // 2 :])
 
     for c in range(ROWS):
-        for h in range(PIECES):
-            @pl.when(gives_far)
-            def _():
+        @pl.when(jnp.logical_and(gives_far, last_y))
+        def _():
+            for h in range(PIECES):
                 to_far(c, h).wait_send()
 
-            @pl.when(gives_next)
-            def _():
-                to_next(c, h).wait_send()
-
-            @pl.when(last_y)
-            def _():
+        @pl.when(jnp.logical_and(gives_far, jnp.logical_not(last_y)))
+        def _():
+            far_row(c).wait_send()
+
+        @pl.when(gives_next)
+        def _():
+            next_row(c).wait_send()
+
+        @pl.when(last_y)
+        def _():
+            for h in range(PIECES):
                 relay(c, h).wait_send()
 
         g = group_of(c)

time: 70.9 us -> 70.4 us (level)
  no operation moved by 1% of the time
where the time goes in v7:
time: 70.4 us; the launch traced here: 70.2 us
  Pallas kernels  69 us (98%)
  local copies, waits for them, and re-layouts  1.28 us (2%)
    pallas_call x1, Pallas kernels, body(): pl.pallas_call(functools.partial(kernel, blocks), out_shape=jax.ShapeDtyp...  69 us

profile of v7, /device:TPU:1, one launch (start us, length us, event | category | flops | bytes accessed | tf_op | source)
XLA Modules:
  0.0 70.2 jit_solution(12573897043155279145)
XLA Ops:
  0.0 69.0 %triangles.1 = f32[8,64]{1,0:T(8,128)} custom-call(s32[16,512]{1,0:T(8,128)} %bitcast.1, bf16[8,8,128,128]{3,2,1,0:T(8,128)(2,1)} %tiles.1), custom_call_target="tpu_custom_call" | custom-call | tf_op jit(solution)/shard_map/triangles/pallas_call | solution.py:588
  69.0 1.3 %copy.4 = f32[8,64]{1,0:T(8,128)} copy(f32[8,64]{1,0:T(8,128)} %triangles.1) | data formatting | bytes 4096
